TPU v7x, 32 devices: a whole 2x2x4 slice. The times are simulated.
32 devices in a mesh: row: 8 (over z, x), col: 4 (over y, core).
Axes of the slice: x: 2, y: 2, z: 4, core: 2. Of those that a mesh axis runs over, the one named last changes fastest.
Arguments:
- momentum: bfloat16 [16384, 16384], P('row', 'col'), may hold values from -16 to 16
- gradient: bfloat16 [16384, 16384], P('row', 'col'), may hold values from -6 to 6
- right_basis: bfloat16 [1024, 16384], P('row', 'col'), may hold values from -1 to 1
Outputs:
- momentum_next: bfloat16 [16384, 16384], P('row', 'col')
- basis_next: float32 [1024, 16384], P('row', 'col')
- update: bfloat16 [16384, 16384], P('row', 'col')
All inputs are finite; a program needn't handle non-finite values.
Results may differ from a plain program's by a relative error of at most 0.02.
Values may be sent and summed in bfloat16 or wider, within the bound.
A program may use at most 128 MiB of HBM per device.

v0:
```python
import math
import jax
import jax.numpy as jnp
from jax import lax
from jax.sharding import PartitionSpec as P

D = 16384
RANK = 1024
momentum_decay = 0.95
epsilon = 1e-06


def orthonormalize(projected, gram_matrix):
    lower_factor = jnp.linalg.cholesky(gram_matrix)
    solved = jax.scipy.linalg.solve_triangular(lower_factor, projected.T, lower=True)
    return solved.T.astype(jnp.bfloat16)


def self_gram(projected):
    return lax.dot_general(
        projected, projected, (((0,), (0,)), ((), ())), precision=lax.Precision.HIGHEST
    )


def body(momentum, gradient, right_basis):
    buffer = (momentum.astype(jnp.float32) + gradient.astype(jnp.float32)).astype(jnp.bfloat16)
    rank_rows = right_basis.shape[0]
    partial_value = lax.dot_general(
        buffer,
        lax.all_gather(right_basis, "row", axis=0, tiled=True),
        (((1,), (1,)), ((), ())),
        preferred_element_type=jnp.float32,
    )
    row_share = lax.psum_scatter(
        partial_value.astype(jnp.bfloat16), "col", scatter_dimension=0, tiled=True
    ).astype(jnp.float32)
    gram_matrix = lax.psum(self_gram(row_share), ("row", "col"))
    ortho_share = orthonormalize(row_share, gram_matrix)
    orthonormal = lax.all_gather(ortho_share, "col", axis=0, tiled=True)
    right_share = lax.psum_scatter(
        lax.dot_general(
            orthonormal, buffer, (((0,), (0,)), ((), ())), preferred_element_type=jnp.float32
        ).astype(jnp.bfloat16),
        "row",
        scatter_dimension=0,
        tiled=True,
    )
    right_wide = right_share.astype(jnp.float32)
    gathered = lax.all_gather(right_share, "row", axis=0, tiled=True)
    gathered_wide = gathered.astype(jnp.float32)
    sums_total = lax.psum(jnp.sum(gathered_wide * gathered_wide, axis=1), "col")
    inverse_norm = lax.rsqrt(sums_total + epsilon)[:, None]
    scaled = (gathered_wide * inverse_norm).astype(jnp.bfloat16)
    feedback = jnp.dot(orthonormal, gathered, preferred_element_type=jnp.float32)
    direction = jnp.dot(orthonormal, scaled, preferred_element_type=jnp.float32)
    offset = lax.axis_index("row") * rank_rows
    basis_next = right_wide * lax.dynamic_slice_in_dim(inverse_norm, offset, rank_rows, 0)
    momentum_next = (buffer.astype(jnp.float32) - (1.0 - momentum_decay) * feedback).astype(
        jnp.bfloat16
    )
    update_scale = D / math.sqrt(RANK)
    update = (update_scale * direction).astype(jnp.bfloat16)
    return (momentum_next, basis_next, update)


def solution(mesh):
    return jax.shard_map(
        body,
        mesh=mesh,
        in_specs=(P("row", "col"), P("row", "col"), P("row", "col")),
        out_specs=(P("row", "col"), P("row", "col"), P("row", "col")),
        check_vma=False,
    )
```

profile of v0, /device:TPU:0, one launch (start us, length us, event | category | flops | bytes accessed | tf_op | source)
XLA Modules:
  0.0 1132.3 jit_solution(6209591932826324028)
XLA Ops:
  7.9 129.4 %all-gather.4.cloned.1.call-done = bf16[1024,4096]{1,0:T(8,128)(2,1)} async-done(((bf16[128,4096]{1,0:T(8,128)(2,1)}), bf16[1024,4096]{1,0:T(8,128)(2,1)}) %all-gather.4.cloned.1.call-update) | async-done | bytes 8388624 | tf_op jit(solution)/shard_map/all_gather | solution.py:30
  137.3 25.8 %convolution_convert_fusion.1 = bf16[2048,1024]{1,0:T(8,128)(2,1)} fusion(bf16[1024,4096]{1,0:T(8,128)(2,1)} %all-gather.4.cloned.1.call-done, bf16[2048,4096]{1,0:T(8,128)(2,1)} %param.4, bf16[2048,4096]{1,0:T(8,128)(2,1)} %param.3), kind=kOutput, calls=%fused_computation.15 | convolution fusion | flops 17215520768 | bytes 46137344 | tf_op jit(solution)/shard_map/dot_general | solution.py:28
  163.2 42.9 %reduce-scatter.3.cloned.1.call-done = bf16[512,1024]{1,0:T(8,128)(2,1)} async-done(((bf16[2048,1024]{1,0:T(8,128)(2,1)}), bf16[512,1024]{1,0:T(8,128)(2,1)}) %reduce-scatter.3.cloned.1.call-update) | async-done | bytes 1048592 | tf_op jit(solution)/shard_map/reduce_scatter | solution.py:34
  206.1 4.9 fusion.67
  211.3 143.2 %all-reduce.3.cloned.1.call-done = f32[1024,1024]{0,1:T(8,128)} async-done(((f32[1024,1024]{0,1:T(8,128)}), f32[1024,1024]{0,1:T(8,128)}) %all-reduce.3.cloned.1.call-update) | async-done | bytes 4194320 | tf_op jit(solution)/shard_map/psum | solution.py:37
  354.5 5.5 copy.7
  366.5 11.7 %cholesky.223 = f32[128,128]{1,0:T(8,128)S(1)} custom-call(f32[128,128]{1,0:T(8,128)S(1)} %cholesky.580), custom_call_target="Cholesky" | custom-call | tf_op jit(solution)/shard_map/jit(cholesky)/cholesky | solution.py:14
  378.2 9.8 custom-call.63
  395.2 12.1 %cholesky.244 = f32[128,128]{1,0:T(8,128)S(1)} custom-call(f32[128,128]{1,0:T(8,128)S(1)} %cholesky.584), custom_call_target="Cholesky" | custom-call | tf_op jit(solution)/shard_map/jit(cholesky)/cholesky | solution.py:14
  408.0 9.8 custom-call.64
  422.7 13.2 %cholesky.468 = f32[128,128]{1,0:T(8,128)} custom-call(f32[128,128]{1,0:T(8,128)} %cholesky.589), custom_call_target="Cholesky" | custom-call | tf_op jit(solution)/shard_map/jit(cholesky)/cholesky | solution.py:14
  438.0 11.3 custom-call.65
  453.6 12.5 %cholesky.487 = f32[128,128]{1,0:T(8,128)} custom-call(f32[128,128]{1,0:T(8,128)S(1)} %cholesky.594), custom_call_target="Cholesky" | custom-call | tf_op jit(solution)/shard_map/jit(cholesky)/cholesky | solution.py:14
  468.2 10.4 custom-call.66
  482.9 11.7 %cholesky.506 = f32[128,128]{1,0:T(8,128)S(1)} custom-call(f32[128,128]{1,0:T(8,128)S(1)} %cholesky.599), custom_call_target="Cholesky" | custom-call | tf_op jit(solution)/shard_map/jit(cholesky)/cholesky | solution.py:14
  495.9 10.0 custom-call.67
  509.2 11.7 %cholesky.526 = f32[128,128]{1,0:T(8,128)S(1)} custom-call(f32[128,128]{1,0:T(8,128)S(1)} %cholesky.604), custom_call_target="Cholesky" | custom-call | tf_op jit(solution)/shard_map/jit(cholesky)/cholesky | solution.py:14
  522.2 9.8 custom-call.68
  535.0 12.0 %cholesky.546 = f32[128,128]{1,0:T(8,128)S(1)} custom-call(f32[128,128]{1,0:T(8,128)S(1)} %cholesky.609), custom_call_target="Cholesky" | custom-call | tf_op jit(solution)/shard_map/jit(cholesky)/cholesky | solution.py:14
  548.4 9.8 custom-call.69
  560.9 11.7 %cholesky.564 = f32[128,128]{1,0:T(8,128)S(1)} custom-call(f32[128,128]{1,0:T(8,128)S(1)} %convolution_subtract_fusion.13), custom_call_target="Cholesky" | custom-call | tf_op jit(solution)/shard_map/jit(cholesky)/cholesky | solution.py:14
  579.5 4.9 select_select_fusion
  584.4 29.0 %while.1 = (s32[]{:T(128)}, f32[1024,1024]{1,0:T(8,128)}, s32[8,2]{0,1:T(2,128)S(1)}, f32[8,128,128]{2,1,0:T(8,128)}, s32[]{:T(128)}) while((s32[]{:T(128)}, f32[1024,1024]{1,0:T(8,128)}, s32[8,2]{0,1:T(2,128)S(1)}, f32[8,128,128]{2,1,0:T(8,128)}, s32[]{:T(128)}) %tuple.57), condition=%wide.while_cond, body=%wide.while_body.sunk | while | flops 2 | bytes 132205 | solution.py:15
  613.4 80.2 %custom-call.70 = f32[8,128,128]{1,2,0:T(8,128)} custom-call(f32[8,128,128]{2,1,0:T(8,128)} %get-tuple-element.10), custom_call_target="InvertDiagBlocksLowerTriangular" | custom-call | tf_op jit(solution)/shard_map/jit(_solve_triangular)/triangular_solve | solution.py:15
  724.2 33.9 %all-gather.6.cloned.1.call-done = bf16[2048,1024]{0,1:T(8,128)(2,1)} async-done(((bf16[512,1024]{0,1:T(8,128)(2,1)}), bf16[2048,1024]{0,1:T(8,128)(2,1)}) %all-gather.6.cloned.1.call-update) | async-done | bytes 4194320 | tf_op jit(solution)/shard_map/all_gather | solution.py:39
  758.1 24.2 %convolution_convert_fusion = bf16[1024,4096]{1,0:T(8,128)(2,1)} fusion(bf16[2048,1024]{0,1:T(8,128)(2,1)} %all-gather.6.cloned.1.call-done, bf16[2048,4096]{1,0:T(8,128)(2,1)} %param.4, bf16[2048,4096]{1,0:T(8,128)(2,1)} %param.3), kind=kOutput, calls=%fused_computation.10 | convolution fusion | flops 17217617920 | bytes 46137344 | tf_op jit(solution)/shard_map/dot_general | solution.py:41
  782.3 147.5 %reduce-scatter.5.cloned.1.call-done = bf16[128,4096]{1,0:T(8,128)(2,1)} async-done(((bf16[1024,4096]{1,0:T(8,128)(2,1)}), bf16[128,4096]{1,0:T(8,128)(2,1)}) %reduce-scatter.5.cloned.1.call-update) | async-done | bytes 1048592 | tf_op jit(solution)/shard_map/reduce_scatter | solution.py:40
  929.9 125.6 %all-gather.8.cloned.1.call-done = bf16[1024,4096]{1,0:T(8,128)(2,1)} async-done(((bf16[128,4096]{1,0:T(8,128)(2,1)}), bf16[1024,4096]{1,0:T(8,128)(2,1)}) %all-gather.8.cloned.1.call-update) | async-done | bytes 8388624 | tf_op jit(solution)/shard_map/all_gather | solution.py:49
  1055.5 5.1 fusion
  1060.5 5.9 psum.15
  1066.5 26.4 %multiply_convert_fusion = bf16[2048,4096]{1,0:T(8,128)(2,1)} fusion(bf16[2048,1024]{0,1:T(8,128)(2,1)} %all-gather.6.cloned.1.call-done, bf16[1024,4096]{1,0:T(8,128)(2,1)} %all-gather.8.cloned.1.call-done, f32[1024]{0:T(1024)S(1)} %add_rsqrt_fusion), kind=kOutput, calls=%fused_computation.2 | convolution fusion | flops 17209229312 | bytes 29364224 | tf_op jit(solution)/shard_map/dot_general | solution.py:55
  1092.9 30.5 %subtract_convert_fusion = bf16[2048,4096]{1,0:T(8,128)(2,1)} fusion(bf16[2048,1024]{0,1:T(8,128)(2,1)S(1)} %copy-done.5, bf16[1024,4096]{1,0:T(8,128)(2,1)} %all-gather.8.cloned.1.call-done, bf16[2048,4096]{1,0:T(8,128)(2,1)} %param.4, bf16[2048,4096]{1,0:T(8,128)(2,1)} %param.3), kind=kOutput, calls=%fused_computation.3 | convolution fusion | flops 17246978048 | bytes 62914560 | tf_op jit(solution)/shard_map/dot_general | solution.py:54
  (115 shorter events, 109.2 us)
Async XLA Ops:
  7.2 130.2 %all-gather.4.cloned.1.call-start = ((), (), s32[]{:S(2)}) async-start(), calls=%async_computation.2 | async-start | bytes 9437184 | tf_op jit(solution)/shard_map/all_gather | solution.py:30
  7.9 198.2 %reduce-scatter.3.cloned.1.call-start = ((), (), s32[]{:S(2)}) async-start(), calls=%async_computation.3 | async-start | bytes 5242880 | tf_op jit(solution)/shard_map/reduce_scatter | solution.py:34
  163.1 191.4 %all-reduce.3.cloned.1.call-start = ((), (), s32[]{:S(2)}) async-start(), calls=%async_computation.4 | async-start | bytes 8388608 | tf_op jit(solution)/shard_map/psum | solution.py:37
  206.1 5.0 copy-start
  211.0 547.1 %all-gather.6.cloned.1.call-start = ((), (), s32[]{:S(2)}) async-start(), calls=%async_computation.5 | async-start | bytes 5242880 | tf_op jit(solution)/shard_map/all_gather | solution.py:39
  364.5 2.0 copy-start.1
  394.5 0.8 copy-start.3
  693.6 7.2 copy-start.4
  724.2 205.7 %reduce-scatter.5.cloned.1.call-start = ((), (), s32[]{:S(2)}) async-start(), calls=%async_computation.6 | async-start | bytes 9437184 | tf_op jit(solution)/shard_map/reduce_scatter | solution.py:40
  782.3 273.2 %all-gather.8.cloned.1.call-start = ((), (), s32[]{:S(2)}) async-start(), calls=%async_computation.7 | async-start | bytes 9437184 | tf_op jit(solution)/shard_map/all_gather | solution.py:49
  1066.5 26.4 %copy-start.5 = (bf16[2048,1024]{0,1:T(8,128)(2,1)S(1)}, bf16[2048,1024]{0,1:T(8,128)(2,1)}, u32[]{:S(2)}) copy-start(bf16[2048,1024]{0,1:T(8,128)(2,1)} %all-gather.6.cloned.1.call-done) | copy-start | bytes 12582916
  1092.9 30.5 %copy-start.2 = (bf16[128,4096]{1,0:T(8,128)(2,1)S(1)}, bf16[128,4096]{1,0:T(8,128)(2,1)}, u32[]{:S(2)}) copy-start(bf16[128,4096]{1,0:T(8,128)(2,1)} %reduce-scatter.5.cloned.1.call-done) | copy-start | bytes 3145732
Sparse Core Ops, SparseCore 0:
  10.1 127.1 all-gather.3
  163.3 42.7 reduce-scatter.2
  212.2 142.2 all-reduce.2
  724.3 33.7 all-gather.5
  782.4 147.4 reduce-scatter.4
  931.9 123.5 all-gather.7
where the time goes:
time: 1140 us; the launch traced here: 1130 us
  waiting for transfers between devices  623 us (55%)
  other arithmetic  275 us (24%)
  matrix products  167 us (15%)
  local copies, waits for them, and re-layouts  41.1 us (4%)
  between operations  19.9 us (2%)
    another operation x30, other arithmetic, orthonormalize(): lower_factor = jnp.linalg.cholesky(gram_matrix)  178 us
    reduce_scatter x1, waiting for transfers between devices, body(): lax.psum_scatter(lax.dot_general(orthonormal, buffer, (((0,), (0,)), ((),...  148 us
    psum x1, waiting for transfers between devices, body(): gram_matrix = lax.psum(self_gram(row_share), ('row', 'col'))  143 us
    all_gather x1, waiting for transfers between devices, body(): lax.all_gather(right_basis, 'row', axis=0, tiled=True)  129 us
    all_gather x1, waiting for transfers between devices, body(): gathered = lax.all_gather(right_share, 'row', axis=0, tiled=True)  126 us
    another operation x3, other arithmetic, orthonormalize(): jax.scipy.linalg.solve_triangular(lower_factor, projected.T, lower=True)  85.1 us
    reduce_scatter x1, waiting for transfers between devices, body(): lax.psum_scatter(partial_value.astype(jnp.bfloat16), 'col', scatter_dimen...  42.9 us
    all_gather x1, waiting for transfers between devices, body(): orthonormal = lax.all_gather(ortho_share, 'col', axis=0, tiled=True)  33.9 us
  transfers between devices with their start and end apart: 6, of which 6 were waited for; matrix products, arithmetic and copies ran while one was open for 0% of the time, Pallas kernels for 0%

commit v1 on v0

--- a/solution.py
+++ b/solution.py
@@ -8,6 +8,18 @@
 RANK = 1024
 momentum_decay = 0.95
 epsilon = 1e-06
+
+
+def collect(array, axis, dim):
+    ways, here, step = (lax.axis_size(axis), lax.axis_index(axis), array.shape[dim])
+    line, have = (array, 1)
+    while have < ways:
+        line = jnp.concatenate(
+            [line, lax.ppermute(line, axis, [(d, (d - have) % ways) for d in range(ways)])],
+            axis=dim,
+        )
+        have = 2 * have
+    return jnp.roll(line, here * step, axis=dim)
 
 
 def orthonormalize(projected, gram_matrix):
@@ -27,7 +39,7 @@
     rank_rows = right_basis.shape[0]
     partial_value = lax.dot_general(
         buffer,
-        lax.all_gather(right_basis, "row", axis=0, tiled=True),
+        collect(right_basis, "row", 0),
         (((1,), (1,)), ((), ())),
         preferred_element_type=jnp.float32,
     )

time: 1140 us -> 1290 us (1.13)
  waiting for transfers between devices: 623 us -> 741 us
  local copies, waits for them, and re-layouts: 41.1 us -> 58.8 us
    ppermute x0 -> x3, waiting for transfers between devices: none -> 244 us  [collect(): lax.ppermute(line, axis, [(d, (d - have) % ways) for d in range(ways)])]
    all_gather x1 -> x0, waiting for transfers between devices: 129 us -> none  [body(): lax.all_gather(right_basis, 'row', axis=0, tiled=True)]
    unnamed x18 -> x31, local copies, waits for them, and re-layouts: 3.26 us -> 16.3 us
  transfers between devices with their start and end apart: 6 -> 8, of which waited for: 6 -> 8; matrix products, arithmetic and copies ran while one was open for 0% -> 0% of each run, Pallas kernels for 0% -> 0%
where the time goes in v1:
time: 1290 us; the launch traced here: 1280 us
  waiting for transfers between devices  741 us (57%)
  other arithmetic  279 us (22%)
  matrix products  167 us (13%)
  local copies, waits for them, and re-layouts  58.8 us (5%)
  between operations  19.6 us (2%)
    ppermute x3, waiting for transfers between devices, collect(): lax.ppermute(line, axis, [(d, (d - have) % ways) for d in range(ways)])  244 us
    another operation x30, other arithmetic, orthonormalize(): lower_factor = jnp.linalg.cholesky(gram_matrix)  178 us
    reduce_scatter x1, waiting for transfers between devices, body(): lax.psum_scatter(lax.dot_general(orthonormal, buffer, (((0,), (0,)), ((),...  148 us
    psum x1, waiting for transfers between devices, body(): gram_matrix = lax.psum(self_gram(row_share), ('row', 'col'))  143 us
    all_gather x1, waiting for transfers between devices, body(): gathered = lax.all_gather(right_share, 'row', axis=0, tiled=True)  126 us
    another operation x3, other arithmetic, orthonormalize(): jax.scipy.linalg.solve_triangular(lower_factor, projected.T, lower=True)  85.1 us
    reduce_scatter x1, waiting for transfers between devices, body(): lax.psum_scatter(partial_value.astype(jnp.bfloat16), 'col', scatter_dimen...  46.5 us
    all_gather x1, waiting for transfers between devices, body(): orthonormal = lax.all_gather(ortho_share, 'col', axis=0, tiled=True)  33.9 us
  transfers between devices with their start and end apart: 8, of which 8 were waited for; matrix products, arithmetic and copies ran while one was open for 0% of the time, Pallas kernels for 0%

profile of v1, /device:TPU:0, one launch (start us, length us, event | category | flops | bytes accessed | tf_op | source)
XLA Modules:
  0.0 1279.6 jit_solution(16016995139956910277)
XLA Ops:
  7.2 6.1 collective-permute-start
  13.3 22.7 %collective-permute-done = bf16[128,4096]{1,0:T(8,128)(2,1)S(1)} collective-permute-done((bf16[128,4096]{1,0:T(8,128)(2,1)}, bf16[128,4096]{1,0:T(8,128)(2,1)S(1)}, u32[]{:S(2)}, u32[]{:S(2)}) %collective-permute-start) | collective-permute-done | bytes 1048608 | tf_op jit(solution)/shard_map/ppermute | solution.py:18
  39.3 45.1 %collective-permute-done.1 = bf16[256,4096]{1,0:T(8,128)(2,1)S(1)} collective-permute-done((bf16[256,4096]{1,0:T(8,128)(2,1)S(1)}, bf16[256,4096]{1,0:T(8,128)(2,1)S(1)}, u32[]{:S(2)}, u32[]{:S(2)}) %collective-permute-start.1) | collective-permute-done | bytes 2097184 | tf_op jit(solution)/shard_map/ppermute | solution.py:18
  91.8 176.5 %collective-permute-done.2 = bf16[512,4096]{1,0:T(8,128)(2,1)} collective-permute-done((bf16[512,4096]{1,0:T(8,128)(2,1)}, bf16[512,4096]{1,0:T(8,128)(2,1)}, u32[]{:S(2)}, u32[]{:S(2)}) %collective-permute-start.2) | collective-permute-done | bytes 4194336 | tf_op jit(solution)/shard_map/ppermute | solution.py:18
  281.2 25.8 %fusion.7 = bf16[2048,1024]{1,0:T(8,128)(2,1)} fusion(bf16[2048,4096]{1,0:T(8,128)(2,1)} %constant_dynamic-update-slice_fusion, s32[]{:T(128)S(6)} %select_n.21, bf16[2048,4096]{1,0:T(8,128)(2,1)} %param.4, bf16[2048,4096]{1,0:T(8,128)(2,1)} %param.3), kind=kOutput, calls=%fused_computation.18 | convolution fusion | flops 17215520768 | bytes 46137348 | tf_op jit(solution)/shard_map/dot_general | solution.py:40
  307.1 46.5 %reduce-scatter.3.cloned.1.call-done = bf16[512,1024]{1,0:T(8,128)(2,1)} async-done(((bf16[2048,1024]{1,0:T(8,128)(2,1)}), bf16[512,1024]{1,0:T(8,128)(2,1)}) %reduce-scatter.3.cloned.1.call-update) | async-done | bytes 1048592 | tf_op jit(solution)/shard_map/reduce_scatter | solution.py:46
  358.8 143.2 %all-reduce.3.cloned.1.call-done = f32[1024,1024]{0,1:T(8,128)} async-done(((f32[1024,1024]{0,1:T(8,128)}), f32[1024,1024]{0,1:T(8,128)}) %all-reduce.3.cloned.1.call-update) | async-done | bytes 4194320 | tf_op jit(solution)/shard_map/psum | solution.py:49
  502.1 5.5 copy.7
  514.1 11.7 cholesky.223
  525.8 9.8 custom-call.63
  542.8 12.1 cholesky.244
  555.5 9.8 custom-call.64
  570.3 13.2 %cholesky.468 = f32[128,128]{1,0:T(8,128)} custom-call(f32[128,128]{1,0:T(8,128)} %cholesky.589), custom_call_target="Cholesky" | custom-call | tf_op jit(solution)/shard_map/jit(cholesky)/cholesky | solution.py:26
  585.6 11.3 custom-call.65
  601.2 12.5 cholesky.487
  615.8 10.4 custom-call.66
  630.5 11.7 cholesky.506
  643.5 10.0 custom-call.67
  656.8 11.7 cholesky.526
  669.8 9.8 custom-call.68
  682.6 12.0 cholesky.546
  696.0 9.8 custom-call.69
  708.4 11.7 cholesky.564
  732.0 29.0 %while.1 = (s32[]{:T(128)}, f32[1024,1024]{1,0:T(8,128)}, s32[8,2]{0,1:T(2,128)S(1)}, f32[8,128,128]{2,1,0:T(8,128)}, s32[]{:T(128)}) while((s32[]{:T(128)}, f32[1024,1024]{1,0:T(8,128)}, s32[8,2]{0,1:T(2,128)S(1)}, f32[8,128,128]{2,1,0:T(8,128)}, s32[]{:T(128)}) %tuple.57), condition=%wide.while_cond, body=%wide.while_body.sunk | while | flops 2 | bytes 132205 | solution.py:27
  761.0 80.2 %custom-call.70 = f32[8,128,128]{1,2,0:T(8,128)} custom-call(f32[8,128,128]{2,1,0:T(8,128)} %get-tuple-element.10), custom_call_target="InvertDiagBlocksLowerTriangular" | custom-call | tf_op jit(solution)/shard_map/jit(_solve_triangular)/triangular_solve | solution.py:27
  871.8 33.9 %all-gather.3.cloned.1.call-done = bf16[2048,1024]{0,1:T(8,128)(2,1)} async-done(((bf16[512,1024]{0,1:T(8,128)(2,1)}), bf16[2048,1024]{0,1:T(8,128)(2,1)}) %all-gather.3.cloned.1.call-update) | async-done | bytes 4194320 | tf_op jit(solution)/shard_map/all_gather | solution.py:51
  905.7 24.2 %convolution_convert_fusion = bf16[1024,4096]{1,0:T(8,128)(2,1)} fusion(bf16[2048,1024]{0,1:T(8,128)(2,1)} %all-gather.3.cloned.1.call-done, bf16[2048,4096]{1,0:T(8,128)(2,1)} %param.4, bf16[2048,4096]{1,0:T(8,128)(2,1)} %param.3), kind=kOutput, calls=%fused_computation.12 | convolution fusion | flops 17217617920 | bytes 46137344 | tf_op jit(solution)/shard_map/dot_general | solution.py:53
  929.9 147.5 %reduce-scatter.5.cloned.1.call-done = bf16[128,4096]{1,0:T(8,128)(2,1)} async-done(((bf16[1024,4096]{1,0:T(8,128)(2,1)}), bf16[128,4096]{1,0:T(8,128)(2,1)}) %reduce-scatter.5.cloned.1.call-update) | async-done | bytes 1048592 | tf_op jit(solution)/shard_map/reduce_scatter | solution.py:52
  1077.5 125.6 %all-gather.5.cloned.1.call-done = bf16[1024,4096]{1,0:T(8,128)(2,1)} async-done(((bf16[128,4096]{1,0:T(8,128)(2,1)}), bf16[1024,4096]{1,0:T(8,128)(2,1)}) %all-gather.5.cloned.1.call-update) | async-done | bytes 8388624 | tf_op jit(solution)/shard_map/all_gather | solution.py:61
  1208.1 5.9 psum.15
  1214.1 26.4 %multiply_convert_fusion = bf16[2048,4096]{1,0:T(8,128)(2,1)} fusion(bf16[2048,1024]{0,1:T(8,128)(2,1)} %all-gather.3.cloned.1.call-done, bf16[1024,4096]{1,0:T(8,128)(2,1)} %all-gather.5.cloned.1.call-done, f32[1024]{0:T(1024)S(1)} %add_rsqrt_fusion), kind=kOutput, calls=%fused_computation.2 | convolution fusion | flops 17209229312 | bytes 29364224 | tf_op jit(solution)/shard_map/dot_general | solution.py:67
  1240.5 30.5 %subtract_convert_fusion = bf16[2048,4096]{1,0:T(8,128)(2,1)} fusion(bf16[2048,1024]{0,1:T(8,128)(2,1)S(1)} %copy-done.8, bf16[1024,4096]{1,0:T(8,128)(2,1)} %all-gather.5.cloned.1.call-done, bf16[2048,4096]{1,0:T(8,128)(2,1)} %param.4, bf16[2048,4096]{1,0:T(8,128)(2,1)} %param.3), kind=kOutput, calls=%fused_computation.3 | convolution fusion | flops 17246978048 | bytes 62914560 | tf_op jit(solution)/shard_map/dot_general | solution.py:66
  (134 shorter events, 147.0 us)
Async XLA Ops:
  7.2 77.2 %copy-start = (bf16[128,4096]{1,0:T(8,128)(2,1)S(1)}, bf16[128,4096]{1,0:T(8,128)(2,1)}, u32[]{:S(2)}) copy-start(bf16[128,4096]{1,0:T(8,128)(2,1)} %param.5) | copy-start | bytes 3145732
  7.2 346.4 %reduce-scatter.3.cloned.1.call-start = ((), (), s32[]{:S(2)}) async-start(), calls=%async_computation.2 | async-start | bytes 5242880 | tf_op jit(solution)/shard_map/reduce_scatter | solution.py:46
  7.2 28.8 %collective-permute-start = (bf16[128,4096]{1,0:T(8,128)(2,1)}, bf16[128,4096]{1,0:T(8,128)(2,1)S(1)}, u32[]{:S(2)}, u32[]{:S(2)}) collective-permute-start(bf16[128,4096]{1,0:T(8,128)(2,1)} %param.5), channel_id=1, source_target_pairs={{0,28},{4,0},{8,4},{12,8},{16,12},{20,16},{24,20},{28,24},{1,29},{... | collective-permute-start | bytes 3145736 | tf_op jit(solution)/shard_map/ppermute | solution.py:18
  36.0 50.6 %copy-start.1 = (bf16[128,4096]{1,0:T(8,128)(2,1)}, bf16[128,4096]{1,0:T(8,128)(2,1)S(1)}, u32[]{:S(2)}) copy-start(bf16[128,4096]{1,0:T(8,128)(2,1)S(1)} %collective-permute-done) | copy-start | bytes 3145732
  37.8 46.6 %collective-permute-start.1 = (bf16[256,4096]{1,0:T(8,128)(2,1)S(1)}, bf16[256,4096]{1,0:T(8,128)(2,1)S(1)}, u32[]{:S(2)}, u32[]{:S(2)}) collective-permute-start(bf16[256,4096]{1,0:T(8,128)(2,1)S(1)} %pad_maximum_fusion.1), channel_id=1, source_target_pairs={{0,24},{4,28},{8,0},{12,4},{16,8},{20,12},{24,16},{28,20},{1,25},{... | collective-permute-start | bytes 6291464 | tf_op jit(solution)/shard_map/ppermute | solution.py:18
  86.6 181.7 %collective-permute-start.2 = (bf16[512,4096]{1,0:T(8,128)(2,1)}, bf16[512,4096]{1,0:T(8,128)(2,1)}, u32[]{:S(2)}, u32[]{:S(2)}) collective-permute-start(bf16[512,4096]{1,0:T(8,128)(2,1)} %pad_maximum_fusion), channel_id=1, source_target_pairs={{0,16},{4,20},{8,24},{12,28},{16,0},{20,4},{24,8},{28,12},{1,17},{... | collective-permute-start | bytes 12582920 | tf_op jit(solution)/shard_map/ppermute | solution.py:18
  91.8 182.2 %copy-start.2 = (bf16[128,4096]{1,0:T(8,128)(2,1)S(1)}, bf16[128,4096]{1,0:T(8,128)(2,1)}, u32[]{:S(2)}) copy-start(bf16[128,4096]{1,0:T(8,128)(2,1)} %copy-done.1) | copy-start | bytes 3145732
  307.0 195.1 %all-reduce.3.cloned.1.call-start = ((), (), s32[]{:S(2)}) async-start(), calls=%async_computation.3 | async-start | bytes 8388608 | tf_op jit(solution)/shard_map/psum | solution.py:49
  353.5 5.0 copy-start.3
  358.5 547.2 %all-gather.3.cloned.1.call-start = ((), (), s32[]{:S(2)}) async-start(), calls=%async_computation.4 | async-start | bytes 5242880 | tf_op jit(solution)/shard_map/all_gather | solution.py:51
  512.1 2.0 copy-start.4
  542.0 0.8 copy-start.6
  841.2 7.2 copy-start.7
  871.8 205.7 %reduce-scatter.5.cloned.1.call-start = ((), (), s32[]{:S(2)}) async-start(), calls=%async_computation.5 | async-start | bytes 9437184 | tf_op jit(solution)/shard_map/reduce_scatter | solution.py:52
  929.9 273.2 %all-gather.5.cloned.1.call-start = ((), (), s32[]{:S(2)}) async-start(), calls=%async_computation.6 | async-start | bytes 9437184 | tf_op jit(solution)/shard_map/all_gather | solution.py:61
  1214.1 26.4 %copy-start.8 = (bf16[2048,1024]{0,1:T(8,128)(2,1)S(1)}, bf16[2048,1024]{0,1:T(8,128)(2,1)}, u32[]{:S(2)}) copy-start(bf16[2048,1024]{0,1:T(8,128)(2,1)} %all-gather.3.cloned.1.call-done) | copy-start | bytes 12582916
  1240.5 30.5 %copy-start.5 = (bf16[128,4096]{1,0:T(8,128)(2,1)S(1)}, bf16[128,4096]{1,0:T(8,128)(2,1)}, u32[]{:S(2)}) copy-start(bf16[128,4096]{1,0:T(8,128)(2,1)} %reduce-scatter.5.cloned.1.call-done) | copy-start | bytes 3145732
Sparse Core Ops, SparseCore 0:
  307.1 46.3 reduce-scatter.2
  359.7 142.3 all-reduce.2
  871.9 33.7 all-gather.2
  930.0 147.4 reduce-scatter.4
  1079.4 123.5 all-gather.4
